TPU v7x, 32 devices: a whole 2x2x4 slice. The times are simulated.
32 devices in a mesh: layer: 4 (over y, core), latent: 8 (over z, x).
Axes of the slice: x: 2, y: 2, z: 4, core: 2. Of those that a mesh axis runs over, the one named last changes fastest.
Arguments:
- inputs: bfloat16 [4, 128, 4096], P('layer', 'latent'), may hold values from -6 to 6
- targets: bfloat16 [4, 128, 4096], P('layer', 'latent'), may hold values from -6 to 6
- w_enc: bfloat16 [4, 4096, 8192], P('layer', None, 'latent'), may hold values from -0.09375 to 0.09375
- b_enc: float32 [4, 8192], P('layer', 'latent'), may hold values from -3 to 3
- w_dec: bfloat16 [4, 4, 8192, 4096], P('layer', None, 'latent'), may hold values from -0.03125 to 0.03125
- b_dec: float32 [4, 4096], P('layer'), may hold values from -3 to 3
Outputs:
- grad_enc: bfloat16 [4, 4096, 8192], P('layer', None, 'latent')
- grad_benc: float32 [4, 8192], P('layer', 'latent')
- grad_dec: bfloat16 [4, 4, 8192, 4096], P('layer', None, 'latent')
- grad_bdec: float32 [4, 4096], P('layer')
All inputs are finite; a program needn't handle non-finite values.
Results may differ from a plain program's by a relative error of at most 0.0057.
Values may be sent and summed in bfloat16 or wider, within the bound.
A program may use at most 192 MiB of HBM per device.

v0:
```python
import jax
import jax.numpy as jnp
from jax import lax
from jax.sharding import PartitionSpec as P

penalty = 0.5
eps = 1e-06


def local(inputs, targets, w_enc, b_enc, w_dec, b_dec):
    source = lax.axis_index("layer")
    depth = w_dec.shape[1]
    whole = lax.all_gather(inputs[0], "latent", axis=0, tiled=True)
    pre = jnp.dot(whole, w_enc[0], preferred_element_type=jnp.float32) + b_enc[0]
    positive = jnp.maximum(pre, 0.0)
    act = (positive * positive).astype(jnp.bfloat16)
    valid = (jnp.arange(depth, dtype=jnp.int32) >= source).astype(jnp.float32)
    partial_value = (
        jnp.einsum("nk,tkd->tnd", act, w_dec[0], preferred_element_type=jnp.float32)
        * valid[:, None, None]
    )
    spread = lax.psum_scatter(partial_value, "layer", scatter_dimension=0, tiled=True)
    recon = lax.psum_scatter(spread, "latent", scatter_dimension=1, tiled=True)
    error = recon[0] + b_dec[0] - targets[0].astype(jnp.float32)
    grad_bdec = lax.psum(jnp.sum(error, axis=0), "latent")[None, :]
    err_low = error.astype(jnp.bfloat16)[None]
    stacked = lax.all_gather(err_low, "latent", axis=1, tiled=True)
    errors = lax.all_gather(stacked, "layer", axis=0, tiled=True)
    errors = jnp.where(valid[:, None, None] > 0.0, errors, jnp.zeros_like(errors))
    decoders = w_dec[0]
    squares = jnp.sum(jnp.square(decoders.astype(jnp.float32)), axis=2)
    norms = jnp.sqrt(jnp.sum(squares * valid[:, None], axis=0) + eps)
    back = jnp.einsum("tnd,tkd->nk", errors, decoders, preferred_element_type=jnp.float32)
    d_act = back + penalty * norms[None, :]
    d_pre = d_act * 2.0 * positive
    grad_benc = jnp.sum(d_pre, axis=0)[None, :]
    d_low = d_pre.astype(jnp.bfloat16)
    grad_enc = lax.dot_general(
        whole, d_low, (((0,), (0,)), ((), ())), preferred_element_type=jnp.float32
    ).astype(jnp.bfloat16)[None]
    act_total = jnp.sum(act.astype(jnp.float32), axis=0)
    scale = penalty * act_total / norms
    grad_mse = jnp.einsum("nk,tnd->tkd", act, errors, preferred_element_type=jnp.float32)
    shrink = valid[:, None, None] * scale[None, :, None] * decoders.astype(jnp.float32)
    grad_dec = (grad_mse + shrink).astype(jnp.bfloat16)[None]
    return (grad_enc, grad_benc, grad_dec, grad_bdec)


def solution(mesh):
    placed = (
        P("layer", "latent", None),
        P("layer", "latent", None),
        P("layer", None, "latent"),
        P("layer", "latent"),
        P("layer", None, "latent", None),
        P("layer", None),
    )
    return jax.shard_map(
        local,
        mesh=mesh,
        in_specs=placed,
        out_specs=(
            P("layer", None, "latent"),
            P("layer", "latent"),
            P("layer", None, "latent", None),
            P("layer", None),
        ),
        check_vma=False,
    )
```

profile of v0, /device:TPU:0, one launch (start us, length us, event | category | flops | bytes accessed | tf_op | source)
XLA Modules:
  0.0 456.9 jit_solution(2697420618974324879)
XLA Ops:
  7.2 0.0 all-gather.9.cloned.1.call-start
  7.2 0.7 all-gather.9.cloned.1.call-update
  7.9 0.0 reduce-scatter.3.cloned.1.call-start
  8.0 45.2 %all-gather.9.cloned.1.call-done = bf16[1,128,4096]{2,1,0:T(8,128)(2,1)} async-done(((bf16[1,16,4096]{2,1,0:T(8,128)(2,1)}), bf16[1,128,4096]{2,1,0:T(8,128)(2,1)}) %all-gather.9.cloned.1.call-update) | async-done | bytes 1048592 | tf_op jit(solution)/shard_map/all_gather | solution.py:13
  53.1 4.9 %convert_reduce_fusion = (f32[1024]{0:T(1024)S(1)}, f32[128,1024]{1,0:T(8,128)S(1)}) fusion(f32[1024]{0:T(1024)} %bitcast.82, bf16[1,4096,1024]{2,1,0:T(8,128)(2,1)} %param.8, bf16[1,128,4096]{2,1,0:T(8,128)(2,1)} %all-gather.9.cloned.1.call-done), kind=kOutput, calls=%fused_computation.23 | convolution fusion | flops 1074527232 | bytes 9969664 | tf_op jit(solution)/shard_map/dot_general | solution.py:14
  58.0 18.5 %multiply_bitcast_fusion = f32[4,128,4096]{2,1,0:T(8,128)} fusion(f32[4]{0:T(128)S(1)} %compare_convert_fusion, bf16[1,4,1024,4096]{3,2,1,0:T(8,128)(2,1)} %param.10, f32[128,1024]{1,0:T(8,128)S(1)} %get-tuple-element.15), kind=kOutput, calls=%fused_computation.13 | convolution fusion | flops 4297326592 | bytes 42467344 | tf_op jit(solution)/shard_map/nk,tkd->tnd/dot_general | solution.py:19
  76.5 0.0 reduce-scatter.3.cloned.1.call-update
  76.6 0.0 reduce-scatter.5.cloned.1.call-start
  76.6 70.2 %reduce-scatter.3.cloned.1.call-done = f32[1,128,4096]{2,1,0:T(8,128)} async-done(((f32[4,128,4096]{2,1,0:T(8,128)}), f32[1,128,4096]{2,1,0:T(8,128)}) %reduce-scatter.3.cloned.1.call-update) | async-done | bytes 2097168 | tf_op jit(solution)/shard_map/reduce_scatter | solution.py:22
  146.9 0.0 reduce-scatter.5.cloned.1.call-update
  146.9 0.0 all-gather.5.cloned.1.call-start
  146.9 72.2 %reduce-scatter.5.cloned.1.call-done = f32[1,16,4096]{2,1,0:T(8,128)} async-done(((f32[1,128,4096]{2,1,0:T(8,128)}), f32[1,16,4096]{2,1,0:T(8,128)}) %reduce-scatter.5.cloned.1.call-update) | async-done | bytes 262160 | tf_op jit(solution)/shard_map/reduce_scatter | solution.py:23
  219.2 0.0 copy-done.2
  219.2 0.0 copy-done.3
  219.2 1.6 fusion.32
  220.8 0.0 all-gather.5.cloned.1.call-update
  220.8 0.0 all-gather.7.cloned.1.call-start
  220.9 40.2 %all-gather.5.cloned.1.call-done = bf16[1,128,4096]{2,1,0:T(8,128)(2,1)} async-done(((bf16[1,16,4096]{2,1,0:T(8,128)(2,1)}), bf16[1,128,4096]{2,1,0:T(8,128)(2,1)}) %all-gather.5.cloned.1.call-update) | async-done | bytes 1048592 | tf_op jit(solution)/shard_map/all_gather | solution.py:27
  261.1 0.0 all-gather.7.cloned.1.call-update
  261.1 40.6 %copy.16 = bf16[1,4,1024,4096]{2,3,1,0:T(8,128)(2,1)} copy(bf16[1,4,1024,4096]{3,2,1,0:T(8,128)(2,1)} %param.10) | data formatting | bytes 67108864 | tf_op args[4]
  301.7 11.7 %fusion = f32[4,1024]{1,0:T(4,128)S(1)} fusion(bf16[1,4,1024,4096]{2,3,1,0:T(8,128)(2,1)} %copy.16), kind=kLoop, calls=%fused_computation.2 | loop fusion | flops 50327552 | bytes 33570816 | tf_op jit(solution)/shard_map/reduce_sum | solution.py:31
  313.4 0.1 multiply_reduce_fusion
  313.5 0.1 broadcast_multiply_fusion
  313.5 0.0 copy-done.1
  313.5 0.1 fusion.34
  313.6 35.7 %psum.7 = f32[1,4096]{1,0:T(1,128)} all-reduce(f32[1,4096]{1,0:T(1,128)S(1)} %bitcast.81), channel_id=1, replica_groups=mesh['layer'=4,'latent'=8] {'latent'}, use_global_device_ids=true, to_apply=%region_7.8 | all-reduce | flops 4096 | bytes 32768 | tf_op jit(solution)/shard_map/psum | solution.py:25
  349.3 25.4 %fusion.7 = bf16[1,4,1024,4096]{2,3,1,0:T(8,128)(2,1)} fusion(bf16[1,4,1024,4096]{2,3,1,0:T(8,128)(2,1)} %copy.16, f32[4,1024]{1,0:T(4,128)S(1)} %broadcast_multiply_fusion, bf16[4,128,4096]{2,1,0:T(8,128)(2,1)} %all-gather.7.cloned.1.call-done, pred[4]{0:T(512)(128)(4,1)S(1)} %broadcast_compare_fusion, f32[128,1024]{1,0:T(8,128)S(1)} %get-tuple-element.15), kind=kOutput, calls=%fused_computation.9 | convolution fusion | flops 4364435456 | bytes 71843840 | tf_op jit(solution)/shard_map/nk,tnd->tkd/dot_general | solution.py:43
  374.7 40.5 %copy.21 = bf16[1,4,1024,4096]{3,2,1,0:T(8,128)(2,1)} copy(bf16[1,4,1024,4096]{2,3,1,0:T(8,128)(2,1)} %fusion.7) | data formatting | bytes 67108864
  415.2 17.6 %fusion.40 = (f32[1024]{0:T(1024)}, bf16[128,1024]{1,0:T(8,128)(2,1)S(1)}) fusion(f32[128,1024]{1,0:T(8,128)S(1)} %get-tuple-element.15, f32[1024]{0:T(1024)S(1)} %get-tuple-element.13, bf16[1,4,1024,4096]{3,2,1,0:T(8,128)(2,1)} %param.10, bf16[4,128,4096]{2,1,0:T(8,128)(2,1)} %all-gather.7.cloned.1.call-done, pred[4]{0:T(512)(128)(4,1)S(1)} %broadcast_compare_fusion), kind=kOutput, calls=%fused_computation.42 | convolution fusion | flops 4297718784 | bytes 38543364 | tf_op jit(solution)/shard_map/tnd,tkd->nk/dot_general | solution.py:33
  432.8 0.0 copy-done
  432.8 5.6 %convert_bitcast_fusion = bf16[1,4096,1024]{1,2,0:T(8,128)(2,1)} fusion(bf16[1,128,4096]{2,1,0:T(8,128)(2,1)S(1)} %copy-done, bf16[128,1024]{1,0:T(8,128)(2,1)S(1)} %get-tuple-element.17), kind=kOutput, calls=%fused_computation.12 | convolution fusion | flops 1077936128 | bytes 9699328 | tf_op jit(solution)/shard_map/dot_general | solution.py:38
  438.4 11.9 %copy.20 = bf16[1,4096,1024]{2,1,0:T(8,128)(2,1)} copy(bf16[1,4096,1024]{1,2,0:T(8,128)(2,1)} %convert_bitcast_fusion) | data formatting | bytes 16777216
  (8 shorter events, 0.0 us)
Async XLA Ops:
  7.2 46.0 %all-gather.9.cloned.1.call-start = ((), (), s32[]{:S(2)}) async-start(), calls=%async_computation.6 | async-start | bytes 1179648 | tf_op jit(solution)/shard_map/all_gather | solution.py:13
  7.9 139.0 %reduce-scatter.3.cloned.1.call-start = ((), (), s32[]{:S(2)}) async-start(), calls=%async_computation.2 | async-start | bytes 10485760 | tf_op jit(solution)/shard_map/reduce_scatter | solution.py:22
  76.5 142.6 %copy-start.2 = (bf16[1,16,4096]{2,1,0:T(8,128)(2,1)S(1)}, bf16[1,16,4096]{2,1,0:T(8,128)(2,1)}, u32[]{:S(2)}) copy-start(bf16[1,16,4096]{2,1,0:T(8,128)(2,1)} %param.7) | copy-start | bytes 393220
  76.5 142.6 %copy-start.3 = (f32[1,4096]{1,0:T(1,128)S(1)}, f32[1,4096]{1,0:T(1,128)}, u32[]{:S(2)}) copy-start(f32[1,4096]{1,0:T(1,128)} %param.11) | copy-start | bytes 49156
  76.6 142.6 %reduce-scatter.5.cloned.1.call-start = ((), (), s32[]{:S(2)}) async-start(), calls=%async_computation.3 | async-start | bytes 2359296 | tf_op jit(solution)/shard_map/reduce_scatter | solution.py:23
  146.9 114.2 %all-gather.5.cloned.1.call-start = ((), (), s32[]{:S(2)}) async-start(), calls=%async_computation.4 | async-start | bytes 1179648 | tf_op jit(solution)/shard_map/all_gather | solution.py:27
  220.8 128.5 %all-gather.7.cloned.1.call-start = ((), (), s32[]{:S(2)}) async-start(), calls=%async_computation.5 | async-start | bytes 5242880 | tf_op jit(solution)/shard_map/all_gather | solution.py:28
  301.6 11.9 %copy-start.1 = (f32[1,16,4096]{2,1,0:T(8,128)S(1)}, f32[1,16,4096]{2,1,0:T(8,128)}, u32[]{:S(2)}) copy-start(f32[1,16,4096]{2,1,0:T(8,128)} %reduce-scatter.5.cloned.1.call-done) | copy-start | bytes 786436
  415.2 17.6 %copy-start = (bf16[1,128,4096]{2,1,0:T(8,128)(2,1)S(1)}, bf16[1,128,4096]{2,1,0:T(8,128)(2,1)}, u32[]{:S(2)}) copy-start(bf16[1,128,4096]{2,1,0:T(8,128)(2,1)} %all-gather.9.cloned.1.call-done) | copy-start | bytes 3145732
Sparse Core Ops, SparseCore 0:
  10.1 42.9 all-gather.8
  76.7 70.1 reduce-scatter.2
  150.4 68.7 reduce-scatter.4
  221.7 39.2 all-gather.4
  262.5 33.1 all-gather.6
where the time goes:
time: 459 us; the launch traced here: 457 us
  waiting for transfers between devices  229 us (50%)
  local copies, waits for them, and re-layouts  93 us (20%)
  matrix products  72 us (16%)
  blocking collectives  35.7 us (8%)
  between operations  13.8 us (3%)
  other arithmetic  13.6 us (3%)
    unnamed x11, local copies, waits for them, and re-layouts  93 us
    reduce_scatter x1, waiting for transfers between devices, local(): recon = lax.psum_scatter(spread, 'latent', scatter_dimension=1, tiled=True)  72.2 us
    reduce_scatter x1, waiting for transfers between devices, local(): lax.psum_scatter(partial_value, 'layer', scatter_dimension=0, tiled=True)  70.2 us
    all_gather x1, waiting for transfers between devices, local(): whole = lax.all_gather(inputs[0], 'latent', axis=0, tiled=True)  45.2 us
    all_gather x1, waiting for transfers between devices, local(): stacked = lax.all_gather(err_low, 'latent', axis=1, tiled=True)  40.2 us
    psum x1, blocking collectives, local(): grad_bdec = lax.psum(jnp.sum(error, axis=0), 'latent')[None, :]  35.7 us
    dot_general x1, matrix products, local(): jnp.einsum('nk,tnd->tkd', act, errors, preferred_element_type=jnp.float32)  25.4 us
    dot_general x1, matrix products, local(): jnp.einsum('nk,tkd->tnd', act, w_dec[0], preferred_element_type=jnp.float32)  18.5 us
  transfers between devices with their start and end apart: 5, of which 4 were waited for; matrix products, arithmetic and copies ran while one was open for 11% of the time, Pallas kernels for 0%

commit v1 on v0

--- a/solution.py
+++ b/solution.py
@@ -5,6 +5,12 @@
 
 penalty = 0.5
 eps = 1e-06
+
+
+def summed_here(array, axis):
+    parts = lax.all_gather(array, axis, axis=0, tiled=False)
+    acc = parts.sum(axis=0)
+    return acc
 
 
 def local(inputs, targets, w_enc, b_enc, w_dec, b_dec):
@@ -22,7 +28,7 @@
     spread = lax.psum_scatter(partial_value, "layer", scatter_dimension=0, tiled=True)
     recon = lax.psum_scatter(spread, "latent", scatter_dimension=1, tiled=True)
     error = recon[0] + b_dec[0] - targets[0].astype(jnp.float32)
-    grad_bdec = lax.psum(jnp.sum(error, axis=0), "latent")[None, :]
+    grad_bdec = summed_here(jnp.sum(error, axis=0), "latent")[None, :]
     err_low = error.astype(jnp.bfloat16)[None]
     stacked = lax.all_gather(err_low, "latent", axis=1, tiled=True)
     errors = lax.all_gather(stacked, "layer", axis=0, tiled=True)

time: 459 us -> 455 us (level)
  blocking collectives: 35.7 us -> 30.9 us
    psum x1 -> x0, blocking collectives: 35.7 us -> none  [local(): grad_bdec = lax.psum(jnp.sum(error, axis=0), 'latent')[None, :]]
    all_gather x0 -> x1, blocking collectives: none -> 30.9 us  [summed_here(): parts = lax.all_gather(array, axis, axis=0, tiled=False)]
  transfers between devices with their start and end apart: 5 -> 5, of which waited for: 4 -> 4; matrix products, arithmetic and copies ran while one was open for 11% -> 12% of each run, Pallas kernels for 0% -> 0%
where the time goes in v1:
time: 455 us; the launch traced here: 453 us
  waiting for transfers between devices  229 us (50%)
  local copies, waits for them, and re-layouts  93 us (20%)
  matrix products  72.1 us (16%)
  blocking collectives  30.9 us (7%)
  other arithmetic  14.2 us (3%)
  between operations  13.8 us (3%)
    unnamed x11, local copies, waits for them, and re-layouts  93 us
    reduce_scatter x1, waiting for transfers between devices, local(): recon = lax.psum_scatter(spread, 'latent', scatter_dimension=1, tiled=True)  72.2 us
    reduce_scatter x1, waiting for transfers between devices, local(): lax.psum_scatter(partial_value, 'layer', scatter_dimension=0, tiled=True)  70.2 us
    all_gather x1, waiting for transfers between devices, local(): whole = lax.all_gather(inputs[0], 'latent', axis=0, tiled=True)  45.2 us
    all_gather x1, waiting for transfers between devices, local(): stacked = lax.all_gather(err_low, 'latent', axis=1, tiled=True)  40.2 us
    all_gather x1, blocking collectives, summed_here(): parts = lax.all_gather(array, axis, axis=0, tiled=False)  30.9 us
    dot_general x1, matrix products, local(): jnp.einsum('nk,tnd->tkd', act, errors, preferred_element_type=jnp.float32)  25.5 us
    dot_general x1, matrix products, local(): jnp.einsum('nk,tkd->tnd', act, w_dec[0], preferred_element_type=jnp.float32)  18.5 us
  transfers between devices with their start and end apart: 5, of which 4 were waited for; matrix products, arithmetic and copies ran while one was open for 12% of the time, Pallas kernels for 0%

profile of v1, /device:TPU:0, one launch (start us, length us, event | category | flops | bytes accessed | tf_op | source)
XLA Modules:
  0.0 452.7 jit_solution(14499993240791043585)
XLA Ops:
  7.2 0.0 all-gather.10.cloned.1.call-start
  7.2 0.7 all-gather.10.cloned.1.call-update
  7.9 0.0 reduce-scatter.3.cloned.1.call-start
  8.0 45.2 %all-gather.10.cloned.1.call-done = bf16[1,128,4096]{2,1,0:T(8,128)(2,1)} async-done(((bf16[1,16,4096]{2,1,0:T(8,128)(2,1)}), bf16[1,128,4096]{2,1,0:T(8,128)(2,1)}) %all-gather.10.cloned.1.call-update) | async-done | bytes 1048592 | tf_op jit(solution)/shard_map/all_gather | solution.py:19
  53.1 4.9 %convert_reduce_fusion = (f32[1024]{0:T(1024)S(1)}, f32[128,1024]{1,0:T(8,128)S(1)}) fusion(f32[1024]{0:T(1024)} %bitcast.82, bf16[1,4096,1024]{2,1,0:T(8,128)(2,1)} %param.8, bf16[1,128,4096]{2,1,0:T(8,128)(2,1)} %all-gather.10.cloned.1.call-done), kind=kOutput, calls=%fused_computation.23 | convolution fusion | flops 1074527232 | bytes 9969664 | tf_op jit(solution)/shard_map/dot_general | solution.py:20
  58.0 18.5 %multiply_bitcast_fusion = f32[4,128,4096]{2,1,0:T(8,128)} fusion(f32[4]{0:T(128)S(1)} %compare_convert_fusion, bf16[1,4,1024,4096]{3,2,1,0:T(8,128)(2,1)} %param.10, f32[128,1024]{1,0:T(8,128)S(1)} %get-tuple-element.19), kind=kOutput, calls=%fused_computation.13 | convolution fusion | flops 4297326592 | bytes 42467344 | tf_op jit(solution)/shard_map/nk,tkd->tnd/dot_general | solution.py:25
  76.5 0.0 reduce-scatter.3.cloned.1.call-update
  76.6 0.0 reduce-scatter.5.cloned.1.call-start
  76.6 70.2 %reduce-scatter.3.cloned.1.call-done = f32[1,128,4096]{2,1,0:T(8,128)} async-done(((f32[4,128,4096]{2,1,0:T(8,128)}), f32[1,128,4096]{2,1,0:T(8,128)}) %reduce-scatter.3.cloned.1.call-update) | async-done | bytes 2097168 | tf_op jit(solution)/shard_map/reduce_scatter | solution.py:28
  146.9 0.0 reduce-scatter.5.cloned.1.call-update
  146.9 0.0 all-gather.6.cloned.1.call-start
  146.9 72.2 %reduce-scatter.5.cloned.1.call-done = f32[1,16,4096]{2,1,0:T(8,128)} async-done(((f32[1,128,4096]{2,1,0:T(8,128)}), f32[1,16,4096]{2,1,0:T(8,128)}) %reduce-scatter.5.cloned.1.call-update) | async-done | bytes 262160 | tf_op jit(solution)/shard_map/reduce_scatter | solution.py:29
  219.2 0.0 copy-done.2
  219.2 0.0 copy-done.3
  219.2 1.6 fusion.32
  220.8 0.0 all-gather.6.cloned.1.call-update
  220.8 0.0 all-gather.8.cloned.1.call-start
  220.9 40.2 %all-gather.6.cloned.1.call-done = bf16[1,128,4096]{2,1,0:T(8,128)(2,1)} async-done(((bf16[1,16,4096]{2,1,0:T(8,128)(2,1)}), bf16[1,128,4096]{2,1,0:T(8,128)(2,1)}) %all-gather.6.cloned.1.call-update) | async-done | bytes 1048592 | tf_op jit(solution)/shard_map/all_gather | solution.py:33
  261.1 0.0 all-gather.8.cloned.1.call-update
  261.1 40.6 %copy.22 = bf16[1,4,1024,4096]{2,3,1,0:T(8,128)(2,1)} copy(bf16[1,4,1024,4096]{3,2,1,0:T(8,128)(2,1)} %param.10) | data formatting | bytes 67108864 | tf_op args[4]
  301.7 11.7 %fusion = f32[4,1024]{1,0:T(4,128)S(1)} fusion(bf16[1,4,1024,4096]{2,3,1,0:T(8,128)(2,1)} %copy.22), kind=kLoop, calls=%fused_computation.2 | loop fusion | flops 50327552 | bytes 33570816 | tf_op jit(solution)/shard_map/reduce_sum | solution.py:37
  313.4 0.1 multiply_reduce_fusion
  313.5 0.1 broadcast_multiply_fusion
  313.5 0.0 copy-done.1
  313.5 0.1 fusion.34
  313.6 30.9 %all-gather.1 = f32[32768]{0:T(1024)S(1)} all-gather(f32[4096]{0:T(1024)S(1)} %fusion.34), channel_id=3, replica_groups=mesh['layer'=4,'latent'=8] {'latent'}, dimensions={0}, use_global_device_ids=true | all-gather | bytes 147456 | tf_op jit(solution)/shard_map/all_gather | solution.py:11
  344.5 0.6 reduce_sum.59
  345.2 25.5 %fusion.7 = bf16[1,4,1024,4096]{2,3,1,0:T(8,128)(2,1)} fusion(bf16[1,4,1024,4096]{2,3,1,0:T(8,128)(2,1)} %copy.22, f32[4,1024]{1,0:T(4,128)S(1)} %broadcast_multiply_fusion, bf16[4,128,4096]{2,1,0:T(8,128)(2,1)} %all-gather.8.cloned.1.call-done, pred[4]{0:T(512)(128)(4,1)S(1)} %broadcast_compare_fusion, f32[128,1024]{1,0:T(8,128)S(1)} %get-tuple-element.19), kind=kOutput, calls=%fused_computation.9 | convolution fusion | flops 4364435456 | bytes 71843840 | tf_op jit(solution)/shard_map/nk,tnd->tkd/dot_general | solution.py:49
  370.6 40.5 %copy.27 = bf16[1,4,1024,4096]{3,2,1,0:T(8,128)(2,1)} copy(bf16[1,4,1024,4096]{2,3,1,0:T(8,128)(2,1)} %fusion.7) | data formatting | bytes 67108864
  411.1 17.6 %fusion.40 = (f32[1024]{0:T(1024)}, bf16[128,1024]{1,0:T(8,128)(2,1)S(1)}) fusion(f32[128,1024]{1,0:T(8,128)S(1)} %get-tuple-element.19, f32[1024]{0:T(1024)S(1)} %get-tuple-element.17, bf16[1,4,1024,4096]{3,2,1,0:T(8,128)(2,1)} %param.10, bf16[4,128,4096]{2,1,0:T(8,128)(2,1)} %all-gather.8.cloned.1.call-done, pred[4]{0:T(512)(128)(4,1)S(1)} %broadcast_compare_fusion), kind=kOutput, calls=%fused_computation.42 | convolution fusion | flops 4297718784 | bytes 38543364 | tf_op jit(solution)/shard_map/tnd,tkd->nk/dot_general | solution.py:39
  428.7 5.6 %convert_bitcast_fusion = bf16[1,4096,1024]{1,2,0:T(8,128)(2,1)} fusion(bf16[1,128,4096]{2,1,0:T(8,128)(2,1)S(1)} %copy-done, bf16[128,1024]{1,0:T(8,128)(2,1)S(1)} %get-tuple-element.21), kind=kOutput, calls=%fused_computation.12 | convolution fusion | flops 1077936128 | bytes 9699328 | tf_op jit(solution)/shard_map/dot_general | solution.py:44
  434.3 11.9 %copy.26 = bf16[1,4096,1024]{2,1,0:T(8,128)(2,1)} copy(bf16[1,4096,1024]{1,2,0:T(8,128)(2,1)} %convert_bitcast_fusion) | data formatting | bytes 16777216
  (10 shorter events, 0.1 us)
Async XLA Ops:
  7.2 46.0 %all-gather.10.cloned.1.call-start = ((), (), s32[]{:S(2)}) async-start(), calls=%async_computation.6 | async-start | bytes 1179648 | tf_op jit(solution)/shard_map/all_gather | solution.py:19
  7.9 139.0 %reduce-scatter.3.cloned.1.call-start = ((), (), s32[]{:S(2)}) async-start(), calls=%async_computation.2 | async-start | bytes 10485760 | tf_op jit(solution)/shard_map/reduce_scatter | solution.py:28
  76.5 142.6 %copy-start.2 = (bf16[1,16,4096]{2,1,0:T(8,128)(2,1)S(1)}, bf16[1,16,4096]{2,1,0:T(8,128)(2,1)}, u32[]{:S(2)}) copy-start(bf16[1,16,4096]{2,1,0:T(8,128)(2,1)} %param.7) | copy-start | bytes 393220
  76.5 142.6 %copy-start.3 = (f32[1,4096]{1,0:T(1,128)S(1)}, f32[1,4096]{1,0:T(1,128)}, u32[]{:S(2)}) copy-start(f32[1,4096]{1,0:T(1,128)} %param.11) | copy-start | bytes 49156
  76.6 142.6 %reduce-scatter.5.cloned.1.call-start = ((), (), s32[]{:S(2)}) async-start(), calls=%async_computation.3 | async-start | bytes 2359296 | tf_op jit(solution)/shard_map/reduce_scatter | solution.py:29
  146.9 114.2 %all-gather.6.cloned.1.call-start = ((), (), s32[]{:S(2)}) async-start(), calls=%async_computation.4 | async-start | bytes 1179648 | tf_op jit(solution)/shard_map/all_gather | solution.py:33
  220.8 124.3 %all-gather.8.cloned.1.call-start = ((), (), s32[]{:S(2)}) async-start(), calls=%async_computation.5 | async-start | bytes 5242880 | tf_op jit(solution)/shard_map/all_gather | solution.py:34
  301.6 11.9 %copy-start.1 = (f32[1,16,4096]{2,1,0:T(8,128)S(1)}, f32[1,16,4096]{2,1,0:T(8,128)}, u32[]{:S(2)}) copy-start(f32[1,16,4096]{2,1,0:T(8,128)} %reduce-scatter.5.cloned.1.call-done) | copy-start | bytes 786436
  411.1 17.6 %copy-start = (bf16[1,128,4096]{2,1,0:T(8,128)(2,1)S(1)}, bf16[1,128,4096]{2,1,0:T(8,128)(2,1)}, u32[]{:S(2)}) copy-start(bf16[1,128,4096]{2,1,0:T(8,128)(2,1)} %all-gather.10.cloned.1.call-done) | copy-start | bytes 3145732
Sparse Core Ops, SparseCore 0:
  10.1 42.9 all-gather.9
  76.7 70.1 reduce-scatter.2
  150.4 68.7 reduce-scatter.4
  221.7 39.2 all-gather.5
  262.5 33.1 all-gather.7
